TPU v7x, 128 devices: a whole 4x4x4 slice. The times are simulated.
128 devices in a mesh: group: 4 (over x), rows: 32 (over z, y, core).
Axes of the slice: x: 4, y: 4, z: 4, core: 2. Of those that a mesh axis runs over, the one named last changes fastest.
Arguments:
- force_rows: float32 [6, 1048576], P(None, ('group', 'rows')), may hold values from -1.5 to 1.5
- owners: int32 [1048576, 1], P(('group', 'rows')), may hold values from 0 to 127; in each aligned block of 8192 rows (0 to 8191, 8192 to 16383, ...) at most 80 rows name the same one
- target: int32 [1048576], P(('group', 'rows')), may hold values from 0 to 255
- rbf_blocks: float32 [128, 256, 256], P(('group', 'rows')), may hold values from -0.375 to 0.375
- displacement: float32 [6, 32768], P(None, ('group', 'rows')), may hold values from -32 to 32
- u_basis: float32 [192, 6, 32768], P(None, None, ('group', 'rows')), may hold values from -3 to 3
- z_basis: float32 [192, 6, 32768], P(None, None, ('group', 'rows')), may hold values from -28 to 28
- v_new: float32 [32, 6, 32768], P(None, None, ('group', 'rows')), may hold values from -32 to 32
- w_new: float32 [32, 6, 32768], P(None, None, ('group', 'rows')), may hold values from -6 to 6
Outputs:
- u_restart: float32 [192, 6, 32768], P(None, None, ('group', 'rows'))
- z_restart: float32 [192, 6, 32768], P(None, None, ('group', 'rows'))
- next_disp: float32 [6, 32768], P(None, ('group', 'rows'))
- wetted_disp: float32 [6, 1048576], P(None, ('group', 'rows'))
Inputs may be any that keep to these rules, and one draw needn't show every extreme that they name: `owners`: at most 80 of the face rows of one device name the same owner device, and some owner device is named by exactly 80 rows of one device in every draw.
All inputs are finite; a program needn't handle non-finite values.
Results may differ from a plain program's by a relative error of at most 0.00007.
Values sent between devices are 32-bit elements; how exact they have to be, the bound alone decides.
A program may use at most 64 MiB of HBM per device.

v0:
```python
import jax
import jax.numpy as jnp
from jax import lax
from jax.sharding import PartitionSpec as P

BLK = 256
K = 192
M = 32


precise = lax.Precision.HIGHEST


def on_device(force_rows, owners, target, rbf_blocks, displacement, u_basis, z_basis, v_new, w_new):
    n_devices = lax.axis_size(("group", "rows"))
    face_count = force_rows.shape[1]
    capacity = 5 * face_count // (4 * n_devices)
    points_dev = displacement.shape[1]
    dof_total = 6 * points_dev * n_devices
    dest_dev = owners[:, 0]
    order_idx = jnp.argsort(dest_dev, stable=True)
    dest_sorted = dest_dev[order_idx]
    starts = jnp.searchsorted(dest_sorted, jnp.arange(n_devices, dtype=jnp.int32))
    slot_rank = jnp.arange(face_count, dtype=jnp.int32) - starts[dest_sorted]
    slot_idx = dest_sorted * capacity + slot_rank
    payload = jnp.concatenate([force_rows, target.astype(jnp.float32)[None, :]], 0)[:, order_idx]
    packed = jnp.zeros((7, n_devices * capacity), jnp.float32).at[:, slot_idx].set(payload)
    arrived = lax.all_to_all(packed, ("group", "rows"), split_axis=1, concat_axis=1, tiled=True)
    spots_idx = arrived[6].astype(jnp.int32)
    point_load = jnp.zeros((6, points_dev), jnp.float32).at[:, spots_idx].add(arrived[:6])
    blocks = point_load.reshape(6, points_dev // BLK, BLK)
    response = jnp.einsum("cbi,bij->cbj", blocks, rbf_blocks, precision=precise).reshape(
        6, points_dev
    )
    residual = response - displacement
    local_dofs = 6 * points_dev
    u_flat = u_basis.reshape(K, local_dofs)
    z_flat = z_basis.reshape(K, local_dofs)
    v_flat = v_new.reshape(M, local_dofs)
    w_flat = w_new.reshape(M, local_dofs)
    r_flat = residual.reshape(local_dofs)
    cross_sum, gram_sum = lax.psum(
        (
            jnp.dot(z_flat, v_flat.T, precision=precise),
            jnp.dot(v_flat, v_flat.T, precision=precise),
        ),
        ("group", "rows"),
    )
    cross_new = cross_sum / dof_total
    gram_new = gram_sum / dof_total
    chol_new = jnp.linalg.cholesky(gram_new)
    new_cols = jax.scipy.linalg.cho_solve((chol_new, True), v_flat)
    jac_v = jnp.dot(cross_new.T, u_flat, precision=precise)
    u_joined = jnp.concatenate([u_flat[M:], w_flat - jac_v], 0)
    z_joined = jnp.concatenate([z_flat[M:], new_cols], 0)
    gram_rest = (
        lax.psum(jnp.dot(z_joined, z_joined.T, precision=precise), ("group", "rows")) / dof_total
    )
    chol_rest = jnp.linalg.cholesky(gram_rest)
    z_restart = jax.scipy.linalg.solve_triangular(chol_rest, z_joined, lower=True)
    step_coef = (
        lax.psum(jnp.dot(z_restart, r_flat, precision=precise), ("group", "rows")) / dof_total
    )
    u_restart = jnp.dot(chol_rest.T, u_joined, precision=precise)
    next_disp = response + jnp.dot(step_coef, u_restart, precision=precise).reshape(6, points_dev)
    outgoing = next_disp[:, spots_idx]
    returned = lax.all_to_all(outgoing, ("group", "rows"), split_axis=1, concat_axis=1, tiled=True)
    wetted_disp = (
        jnp.zeros((6, face_count), jnp.float32).at[:, order_idx].set(returned[:, slot_idx])
    )
    return (
        u_restart.reshape(K, 6, points_dev),
        z_restart.reshape(K, 6, points_dev),
        next_disp,
        wetted_disp,
    )


def solution(mesh):
    return jax.shard_map(
        on_device,
        mesh=mesh,
        in_specs=(
            P(None, ("group", "rows")),
            P(("group", "rows"), None),
            P(("group", "rows")),
            P(("group", "rows"), None, None),
            P(None, ("group", "rows")),
            P(None, None, ("group", "rows")),
            P(None, None, ("group", "rows")),
            P(None, None, ("group", "rows")),
            P(None, None, ("group", "rows")),
        ),
        out_specs=(
            P(None, None, ("group", "rows")),
            P(None, None, ("group", "rows")),
            P(None, ("group", "rows")),
            P(None, ("group", "rows")),
        ),
        check_vma=False,
    )
```

profile of v0, /device:TPU:1, one launch (start us, length us, event | category | flops | bytes accessed | tf_op | source)
XLA Modules:
  0.0 639.7 jit_solution(763344193309272180)
XLA Ops:
  8.6 68.8 %psum.28 = f32[32,32]{0,1:T(8,128)S(1)} all-reduce(f32[32,32]{0,1:T(8,128)S(1)} %convolution_bitcast_fusion.1), channel_id=1, replica_groups=mesh['group'=4,'rows'=32] {'group','rows'}, use_global_device_ids=true, to_apply=%region_0.0 | all-reduce | flops 1024 | bytes 8192 | tf_op jit(solution)/shard_map/psum | solution.py:42
  77.4 2.9 cholesky.66
  81.7 2.4 custom-call.25
  87.3 1.8 fusion.10
  89.2 6.8 %sort.17 = (s32[8192]{0:T(1024)}, s32[8192]{0:T(1024)S(1)}) sort(s32[8192]{0:T(1024)S(1)} %bitcast.99, s32[8192]{0:T(1024)S(1)} %iota.114), dimensions={0}, to_apply=%region_9.10 | sort | flops 106496 | bytes 131072 | tf_op jit(solution)/shard_map/jit(argsort)/sort | solution.py:21
  96.5 45.5 %gather_fusion.1 = s32[8192]{0:T(1024)S(1)} fusion(s32[8192]{0:T(1024)S(1)} %bitcast.100, s32[8192]{0:T(1024)S(1)} %get-tuple-element.140), kind=kCustom, calls=%fused_computation.1 | custom fusion | bytes 98304 | tf_op jit(solution)/shard_map/gather | solution.py:22
  142.1 17.0 %while.26 = (s32[]{:T(128)}, u32[128]{0:T(128)S(1)}, u32[128]{0:T(128)S(1)}, s32[8192]{0:T(1024)S(1)}, s32[]{:T(128)}, /*index=5*/s32[]{:T(128)}, s32[]{}) while((s32[]{:T(128)}, u32[128]{0:T(128)S(1)}, u32[128]{0:T(128)S(1)}, s32[8192]{0:T(1024)S(1)}, s32[]{:T(128)}, /*index=5*/s32[]{:T(128)}, s32[]{}) %tuple.56), condition=%wide.region_11.12_spmd.clone, body=%wide.region_10.11_spmd.clone.sunk | while | flops 2692 | bytes 10340 | solution.py:23
  159.2 48.9 %gather_fusion.2 = s32[8192]{0:T(1024)S(1)} fusion(s32[128]{0:T(128)S(1)} %convert_element_type.26, s32[8192]{0:T(1024)S(1)} %broadcast_clamp_fusion.2), kind=kCustom, calls=%fused_computation.2 | custom fusion | bytes 98304 | tf_op jit(solution)/shard_map/gather | solution.py:24
  208.3 2.7 copy.68
  211.0 69.6 %scatter_custom_fusion = f32[7,10240]{0,1:T(8,128)} fusion(s32[8192]{0:T(1024)S(1)} %bitcast.125, f32[7,8192]{0,1:T(8,128)} %copy.68, s32[8192]{0:T(1024)S(1)} %get-tuple-element.140, f32[]{:T(128)} %constant.174.clone.1), kind=kCustom, calls=%fused_computation.19 | custom fusion | bytes 287232 | tf_op jit(solution)/shard_map/scatter | solution.py:27
  280.7 4.3 copy.69
  284.9 5.4 all-to-all-start
  290.4 1.7 convolution_bitcast_fusion
  295.2 1.4 copy.88
  296.6 1.7 copy.87
  301.4 11.7 %cholesky.125 = f32[128,128]{1,0:T(8,128)S(1)} custom-call(f32[128,128]{1,0:T(8,128)S(1)} %cholesky.159), custom_call_target="Cholesky" | custom-call | tf_op jit(solution)/shard_map/jit(cholesky)/cholesky | solution.py:59
  313.2 9.8 %custom-call.26 = f32[1,128,128]{1,2,0:T(8,128)S(1)} custom-call(f32[1,128,128]{2,1,0:T(8,128)S(1)} %get-tuple-element.138), custom_call_target="InvertDiagBlocksLowerTriangular" | custom-call | tf_op jit(solution)/shard_map/jit(cholesky)/cholesky | solution.py:59
  323.4 5.8 cholesky.145
  332.1 20.4 %custom-call.27 = f32[2,128,128]{1,2,0:T(8,128)} custom-call(f32[2,128,128]{2,1,0:T(8,128)S(1)} %pad_maximum_fusion.2), custom_call_target="InvertDiagBlocksLowerTriangular" | custom-call | tf_op jit(solution)/shard_map/jit(_solve_triangular)/triangular_solve | solution.py:60
  352.6 2.0 fusion.26
  357.2 1.4 fusion.25
  361.0 4.0 copy.71
  365.7 55.1 %scatter_custom_fusion.1 = f32[6,256]{0,1:T(8,128)S(1)} fusion(s32[10240]{0:T(1024)} %bitcast.124, f32[10240,6]{1,0:T(8,128)} %copy.71, f32[]{:T(128)} %constant.174.clone.1), kind=kCustom, calls=%fused_computation.69 | custom fusion | flops 61440 | bytes 6656 | tf_op jit(solution)/shard_map/scatter-add | solution.py:30
  422.3 69.8 %all-reduce.3 = (f32[192,32]{0,1:T(8,128)S(1)}, f32[192]{0:T(256)S(1)}) all-reduce(f32[192,32]{0,1:T(8,128)S(1)} %copy-done.14, f32[192]{0:T(256)S(1)} %bitcast.131), channel_id=1, replica_groups=mesh['group'=4,'rows'=32] {'group','rows'}, use_global_device_ids=true, to_apply=%region_8.9 | all-reduce | flops 6336 | bytes 50688 | tf_op jit(solution)/shard_map/psum | solution.py:42
  492.9 2.4 fusion.14
  496.2 37.5 %gather_fusion.3 = f32[10240,6]{1,0:T(8,128)} fusion(f32[6,256]{0,1:T(8,128)S(1)} %copy.72, s32[10240]{0:T(1024)} %broadcast_clamp_fusion), kind=kCustom, calls=%fused_computation.4 | custom fusion | bytes 532480 | tf_op jit(solution)/shard_map/gather | solution.py:66
  533.7 3.4 copy.73
  538.5 5.8 all-to-all-start.1
  546.7 8.4 %all-to-all-done.1 = f32[128,1,480]{2,1,0:T(1,128)S(1)} async-done(((f32[128,1,480]{2,1,0:T(1,128)}), f32[128,1,480]{2,1,0:T(1,128)S(1)}, u32[]{:S(2)}, u32[]{:S(2)}) %all-to-all-start.1) | async-done | bytes 245792 | tf_op jit(solution)/shard_map/all_to_all | solution.py:67
  557.0 3.2 copy.74
  560.2 68.9 %scatter_custom_fusion.2 = f32[6,8192]{0,1:T(8,128)} fusion(s32[8192]{0:T(1024)} %get-tuple-element.139, f32[6,10240]{0,1:T(8,128)} %bitcast.108, s32[8192]{0:T(1024)} %broadcast_clamp_fusion.1, f32[]{:T(128)} %constant.174.clone.1), kind=kCustom, calls=%fused_computation.17 | custom fusion | bytes 197120 | tf_op jit(solution)/shard_map/scatter | solution.py:69
  629.1 3.5 copy.77
  (165 shorter events, 45.6 us)
Async XLA Ops:
  7.2 413.7 %copy-start = (f32[1,256,256]{2,1,0:T(8,128)S(1)}, f32[1,256,256]{2,1,0:T(8,128)}, u32[]{:S(2)}) copy-start(f32[1,256,256]{2,1,0:T(8,128)} %param.14) | copy-start | bytes 786436
  7.2 82.0 %copy-start.1 = (s32[8192,1]{0,1:T(1,128)S(1)}, s32[8192,1]{0,1:T(1,128)}, u32[]{:S(2)}) copy-start(s32[8192,1]{0,1:T(1,128)} %param.12) | copy-start | bytes 98308
  7.2 292.2 %all-reduce.6.cloned.1.call-start = ((), (), s32[]{:S(2)}) async-start(), calls=%async_computation.2 | async-start | bytes 393216 | tf_op jit(solution)/shard_map/psum | solution.py:57
  85.8 10.8 %copy-start.6 = (f32[32,1536]{1,0:T(8,128)}, f32[32,1536]{1,0:T(8,128)S(1)}, u32[]{:S(2)}) copy-start(f32[32,1536]{1,0:T(8,128)S(1)} %fusion.37) | copy-start | bytes 589828
  159.2 49.0 %copy-start.16 = (s32[8192]{0:T(1024)S(1)}, s32[8192]{0:T(1024)}, u32[]{:S(2)}) copy-start(s32[8192]{0:T(1024)} %param.13) | copy-start | bytes 98308
  159.2 49.0 %copy-start.12 = (f32[6,8192]{1,0:T(8,128)S(1)}, f32[6,8192]{1,0:T(8,128)}, u32[]{:S(2)}) copy-start(f32[6,8192]{1,0:T(8,128)} %param.11) | copy-start | bytes 589828
  280.6 9.7 %copy-start.2 = (f32[192,6,256]{2,0,1:T(8,128)S(1)}, f32[192,6,256]{2,0,1:T(8,128)}, u32[]{:S(2)}) copy-start(f32[192,6,256]{2,0,1:T(8,128)} %param.17) | copy-start | bytes 3538948
  280.6 9.7 %copy-start.5 = (f32[32,6,256]{2,0,1:T(8,128)S(1)}, f32[32,6,256]{2,0,1:T(8,128)}, u32[]{:S(2)}) copy-start(f32[32,6,256]{2,0,1:T(8,128)} %param.18) | copy-start | bytes 589828
  280.7 12.1 %slice-start = ((f32[192,6,256]{2,0,1:T(8,128)}), f32[128,6,256]{2,0,1:T(8,128)S(1)}, s32[]{:S(2)}) async-start(f32[192,6,256]{2,0,1:T(8,128)} %param.17), calls=%async_computation.3 | async-start | bytes 1572864 | tf_op jit(solution)/shard_map/jit(_solve_triangular)/triangular_solve | solution.py:60
  284.9 72.3 %all-to-all-start = ((f32[7,128,80]{2,0,1:T(8,128)}), f32[7,128,80]{2,0,1:T(8,128)}, u32[]{:S(2)}, u32[]{:S(2)}) async-start(f32[7,128,80]{2,0,1:T(8,128)} %copy.69), calls=%async_computation | async-start | bytes 1048576 | tf_op jit(solution)/shard_map/all_to_all | solution.py:28
  296.6 58.0 %copy-start.7 = (f32[32,1536]{1,0:T(8,128)S(1)}, f32[32,1536]{1,0:T(8,128)}, u32[]{:S(2)}) copy-start(f32[32,1536]{1,0:T(8,128)} %copy-done.6) | copy-start | bytes 589828
  329.2 23.3 %copy-start.8 = (f32[192,192]{1,0:T(8,128)}, f32[192,192]{1,0:T(8,128)S(1)}, u32[]{:S(2)}) copy-start(f32[192,192]{1,0:T(8,128)S(1)} %get-tuple-element.142) | copy-start | bytes 442372
  332.0 20.6 %copy-start.11 = (f32[192,192]{1,0:T(8,128)}, f32[192,192]{1,0:T(8,128)S(1)}, u32[]{:S(2)}) copy-start(f32[192,192]{1,0:T(8,128)S(1)} %fusion.21) | copy-start | bytes 442372
  357.2 65.1 %copy-start.3 = (f32[64,1536]{1,0:T(8,128)}, f32[64,1536]{1,0:T(8,128)S(1)}, u32[]{:S(2)}) copy-start(f32[64,1536]{1,0:T(8,128)S(1)} %fusion.33) | copy-start | bytes 1179652
  357.2 64.0 %copy-start.17 = (f32[6,256]{1,0:T(8,128)S(1)}, f32[6,256]{1,0:T(8,128)}, u32[]{:S(2)}) copy-start(f32[6,256]{1,0:T(8,128)} %param.15) | copy-start | bytes 18436
  358.8 6.2 copy-start.13
  360.0 132.1 %copy-start.10 = (f32[6,4,8,256]{3,2,0,1:T(8,128)S(1)}, f32[6,4,8,256]{3,2,0,1:T(8,128)}, u32[]{:S(2)}) copy-start(f32[6,4,8,256]{3,2,0,1:T(8,128)} %copy.87) | copy-start | bytes 589828
  361.0 61.3 %copy-start.14 = (f32[192,32]{0,1:T(8,128)S(1)}, f32[192,32]{0,1:T(8,128)}, u32[]{:S(2)}) copy-start(f32[192,32]{0,1:T(8,128)} %convolution_bitcast_fusion) | copy-start | bytes 73732
  361.0 131.9 %copy-start.9 = (f32[192,192]{1,0:T(8,128)S(1)}, f32[192,192]{1,0:T(8,128)}, u32[]{:S(2)}) copy-start(f32[192,192]{1,0:T(8,128)} %copy-done.8) | copy-start | bytes 442372
  496.0 41.1 %copy-start.15 = (f32[6,256]{1,0:T(8,128)}, f32[6,256]{1,0:T(8,128)S(1)}, u32[]{:S(2)}) copy-start(f32[6,256]{1,0:T(8,128)S(1)} %add.123) | copy-start | bytes 18436
  533.7 10.6 %copy-start.4 = (f32[64,1536]{1,0:T(8,128)S(1)}, f32[64,1536]{1,0:T(8,128)}, u32[]{:S(2)}) copy-start(f32[64,1536]{1,0:T(8,128)} %copy-done.3) | copy-start | bytes 1179652
  538.5 16.5 %all-to-all-start.1 = ((f32[128,1,480]{2,1,0:T(1,128)}), f32[128,1,480]{2,1,0:T(1,128)S(1)}, u32[]{:S(2)}, u32[]{:S(2)}) async-start(f32[128,1,480]{2,1,0:T(1,128)} %reshape.292), calls=%async_computation.1 | async-start | bytes 524288 | tf_op jit(solution)/shard_map/all_to_all | solution.py:67
Sparse Core Ops, SparseCore 0:
  89.2 140.9 all-reduce.5
where the time goes:
time: 651 us; the launch traced here: 640 us
  local copies, waits for them, and re-layouts  324 us (50%)
  blocking collectives  139 us (21%)
  other arithmetic  125 us (19%)
  between operations  16.3 us (3%)
  matrix products  15.7 us (2%)
  starting transfers between devices  11.2 us (2%)
  waiting for transfers between devices  8.4 us (1%)
    psum x2, blocking collectives, on_device(): lax.psum((jnp.dot(z_flat, v_flat.T, precision=precise), jnp.dot(v_flat, v...  139 us
    scatter x1, local copies, waits for them, and re-layouts, on_device(): jnp.zeros((7, n_devices * capacity), jnp.float32).at[:, slot_idx]  69.6 us
    scatter x1, local copies, waits for them, and re-layouts, on_device(): jnp.zeros((6, face_count), jnp.float32).at[:, order_idx]  68.9 us
    scatter-add x1, other arithmetic, on_device(): jnp.zeros((6, points_dev), jnp.float32).at[:, spots_idx].add(arrived[:6])  55.1 us
    gather x1, local copies, waits for them, and re-layouts, on_device(): slot_rank = jnp.arange(face_count, dtype=jnp.int32) - starts[dest_sorted]  48.9 us
    gather x1, local copies, waits for them, and re-layouts, on_device(): dest_sorted = dest_dev[order_idx]  45.5 us
    gather x1, local copies, waits for them, and re-layouts, on_device(): outgoing = next_disp[:, spots_idx]  37.5 us
    another operation x7, other arithmetic, on_device(): chol_rest = jnp.linalg.cholesky(gram_rest)  28.8 us
  transfers between devices with their start and end apart: 3, of which 1 were waited for; matrix products, arithmetic and copies ran while one was open for 41% of the time, Pallas kernels for 0%

commit v1 on v0

v1 whole, which is shorter than its diff:
```python
import functools

import jax
import jax.numpy as jnp
from jax import lax
from jax.experimental import pallas as pl
from jax.experimental.pallas import tpu as pltpu
from jax.sharding import PartitionSpec as P

BLK = 256
K = 192
M = 32
KEEP = K - M
NB = 32
ROWS = K + M
GBLK = ROWS // 8
FACE_CHUNK = 512

MESH = pl.DeviceIdType.MESH
F32 = jnp.float32
BF16 = jnp.bfloat16
AXES = ("group", "rows")


def iota(shape, dim):
    return lax.broadcasted_iota(jnp.int32, shape, dim)


def dot(a, b, dims):
    return lax.dot_general(
        a, b, (dims, ((), ())), precision=lax.Precision.HIGHEST, preferred_element_type=F32
    )


def nn(a, b):
    return dot(a, b, ((1,), (0,)))


def nt(a, b):
    return dot(a, b, ((1,), (1,)))


def tn(a, b):
    return dot(a, b, ((0,), (0,)))


def split(x):
    high = x.astype(BF16)
    return high, (x - high.astype(F32)).astype(BF16)


def eliminate(panel, first):
    rows = iota((NB, 1), 0)
    for j in range(NB):
        at = first + j
        pivot_row = panel[j : j + 1, :]
        inverse = 1.0 / pivot_row[:, at : at + 1]
        factor = jnp.where(rows > j, panel[:, at : at + 1] * inverse, 0.0)
        panel = panel - factor * pivot_row
    own = iota(panel.shape, 1) == first + iota(panel.shape, 0)
    pivots = jnp.sum(jnp.where(own, panel, 0.0), axis=1, keepdims=True)
    return panel * lax.rsqrt(pivots)


def exchange_kernel(
    n_g, n_r,
    force, owner, target, rbf, disp, u, z, v, w,
    table_hi, table_lo, mix_u, mix_z, next_disp,
    gram_send, gram_recv, gram_sum, gram_all,
    load, load_recv, q_send, q_recv, disp_send, table,
    aug, coef_scr,
    gs_sem, gr_sem, ga_send_sem, ga_sem, ls_sem, lr_sem, qs_sem, qr_sem, ts_sem, tr_sem,
):
    n = n_g * n_r
    me = lax.axis_index("group") * n_r + lax.axis_index("rows")
    reducers = min(n, GBLK)
    stride = n // 32 if n >= 32 else 1
    slots = -(-GBLK // reducers)
    dof_total = 6 * BLK * n

    def device(p):
        return (p // n_r, lax.rem(p, n_r))

    def others(body):
        def step(k, carry):
            body(lax.rem(me + k, n))
            return carry

        lax.fori_loop(1, n, step, 0)

    def remote(src, dst, send, recv, p):
        return pltpu.make_async_remote_copy(
            src_ref=src, dst_ref=dst, send_sem=send, recv_sem=recv,
            device_id=device(p), device_id_type=MESH,
        )

    barrier = pltpu.get_barrier_semaphore()
    others(lambda p: pl.semaphore_signal(barrier, inc=1, device_id=device(p), device_id_type=MESH))

    gram = jnp.zeros((ROWS, ROWS), F32)
    for c in range(6):
        joined = jnp.concatenate([z[c, M:, :], v[c], z[c, :M, :]], 0)
        gram = gram + nt(joined, joined)
    gram = gram * (1.0 / dof_total)
    gram = jnp.concatenate([gram, jnp.zeros((ROWS, 256 - ROWS), F32)], 1)
    gram_send[...] = gram.reshape(GBLK, 8, 256)

    pl.semaphore_wait(barrier, n - 1)

    def gram_blocks(away, here):
        def step(b, carry):
            slot, p = b // reducers, lax.rem(b, reducers) * stride

            @pl.when(p != me)
            def _():
                away(b, slot, p)

            if here is not None:

                @pl.when(p == me)
                def _():
                    here(b, slot)

            return carry

        lax.fori_loop(0, GBLK, step, 0)

    def gram_copy(b, slot, p):
        return remote(gram_send.at[b], gram_recv.at[slot, me], gs_sem, gr_sem.at[slot], p)

    gram_blocks(
        lambda b, slot, p: gram_copy(b, slot, p).start(),
        lambda b, slot: pltpu.make_async_copy(
            gram_send.at[b], gram_recv.at[slot, me], gr_sem.at[slot]
        ).start(),
    )

    def reducing(body):
        for slot in range(slots):
            b = slot * reducers + me // stride

            @pl.when((lax.rem(me, stride) == 0) & (me // stride < reducers) & (b < GBLK))
            def _():
                body(slot, b)

    faces = force.shape[1]
    chunk = min(FACE_CHUNK, faces)
    load[...] = jnp.zeros_like(load)

    def scatter(i, carry):
        at = pl.ds(pl.multiple_of(i * chunk, chunk), chunk)
        at_owner = (iota((n, chunk), 0) == owner[:, at]).astype(F32).astype(BF16)
        at_point = (iota((BLK, chunk), 0) == target[:, at]).astype(F32).astype(BF16)
        high, low = split(force[:, at])
        left = jnp.concatenate(
            [
                jnp.concatenate([at_owner * high[c : c + 1], at_owner * low[c : c + 1]], 1)
                for c in range(6)
            ],
            0,
        )
        right = jnp.concatenate([at_point, at_point], 1)
        add = lax.dot_general(left, right, (((1,), (1,)), ((), ())), preferred_element_type=F32)
        load[...] += add.reshape(6, n, BLK)
        return carry

    half = faces // chunk // 2
    lax.fori_loop(0, half, scatter, 0)

    def reduce_gram(slot, b):
        pltpu.make_async_copy(gram_recv.at[slot], gram_recv.at[slot], gr_sem.at[slot]).wait()
        gram_sum[slot] = jnp.sum(gram_recv[slot], axis=0)

    reducing(reduce_gram)

    def share_gram(slot, b):
        others(lambda p: remote(gram_sum.at[slot], gram_all.at[b], ga_send_sem, ga_sem, p).start())
        pltpu.make_async_copy(gram_sum.at[slot], gram_all.at[b], ga_sem).start()

    reducing(share_gram)

    lax.fori_loop(half, faces // chunk, scatter, 0)

    def row(ref, p):
        return ref.at[:, pl.ds(p, 1), :]

    def load_copy(p):
        return remote(row(load, p), row(load_recv, me), ls_sem, lr_sem, p)

    others(lambda p: load_copy(p).start())
    pltpu.make_async_copy(row(load, me), row(load_recv, me), lr_sem).start()

    pltpu.make_async_copy(gram_all, gram_all, ga_sem).wait()
    total = gram_all[...].reshape(ROWS, 256)

    lane32 = iota((NB, 128), 1)
    row32 = iota((NB, 128), 0)
    start = jnp.where(
        (lane32 >= 32) & (lane32 < 64), total[KEEP:K, 128:], jnp.where(lane32 - 64 == row32, 1.0, 0.0)
    )
    factor = eliminate(start, 32)
    factor = pltpu.roll(factor, 96, 1)
    factor = jnp.where((lane32 >= 32) & (lane32 < 64), factor, 0.0)
    inverse = tn(factor, factor)
    scaled = nn(total[:, 128:], inverse)

    lanes = iota((ROWS, 256), 1)
    index = iota((ROWS, 256), 0)
    new_lane = (lanes >= KEEP) & (lanes < K)
    new_row = (index >= KEEP) & (index < K)
    scaled = jnp.concatenate([jnp.zeros((ROWS, 128), F32), scaled], 1)
    inverse_rows = jnp.concatenate(
        [jnp.zeros((KEEP, 128), F32), inverse[32:64], jnp.zeros((M, 128), F32)], 0
    )
    inverse_full = jnp.concatenate([jnp.zeros((ROWS, 128), F32), inverse_rows], 1)
    unit = jnp.where(lanes == index, 1.0, 0.0)
    matrix = jnp.where(new_lane, jnp.where(new_row, inverse_full, scaled), total)
    matrix = jnp.where(lanes < K, matrix, 0.0)
    extra = jnp.where(new_lane, inverse_full, unit)
    aug[:, 0:256] = matrix[:K]
    aug[:, 256:512] = extra[:K]
    coef = jnp.where(new_lane, jnp.where(new_row, inverse_full, -scaled), jnp.where(lanes < KEEP, unit, 0.0))
    coef_scr[...] = coef
    change = jnp.where(lanes == index, 1.0, jnp.where(new_row & (lanes < ROWS), -total, 0.0))
    change = jnp.where(new_row & new_lane, unit, change)
    change = jnp.where(index < K, change, 0.0)

    def block(b):
        r0 = b * NB
        panel = aug[r0 : r0 + NB, :]
        lane = iota((NB, 512), 1)
        done = eliminate(panel, r0)
        done = jnp.where(lane < r0, 0.0, done)
        aug[r0 : r0 + NB, :] = done
        if r0 + NB < K:
            first = 128 if r0 + NB >= 128 else 0
            update = tn(done[:, first:256], done)
            aug[r0 + NB : K, :] = aug[r0 + NB : K, :] - update[r0 + NB - first : K - first, :]

    block(0)
    block(1)

    pltpu.make_async_copy(load_recv, load_recv, lr_sem).wait()
    point_load = jnp.concatenate(
        [jnp.sum(load_recv[c], axis=0, keepdims=True) for c in range(6)], 0
    )
    response = nn(point_load, rbf[...])
    residual = response - disp[...]
    disp_send[...] = response.reshape(6, 1, BLK)
    weighted = jnp.zeros((K, BLK), F32)
    for c in range(6):
        kept = jnp.concatenate([z[c, M:, :], v[c]], 0)
        weighted = weighted + kept * residual[c : c + 1]
    q_column = jnp.sum(weighted, axis=1, keepdims=True) * (1.0 / dof_total)
    diagonal = iota((K, 256), 0) == iota((K, 256), 1)
    q_send[...] = jnp.sum(jnp.where(diagonal, q_column, 0.0), axis=0, keepdims=True)

    def q_copy(p):
        return remote(q_send, q_recv.at[me], qs_sem, qr_sem, p)

    others(lambda p: q_copy(p).start())
    pltpu.make_async_copy(q_send, q_recv.at[me], qr_sem).start()

    block(2)
    block(3)

    pltpu.make_async_copy(q_recv, q_recv, qr_sem).wait()
    q_row = jnp.sum(q_recv[...], axis=0)
    step_coef = jnp.sum(coef_scr[...] * q_row, axis=1, keepdims=True)
    for c in range(6):
        joined = jnp.concatenate([u[c, M:, :], w[c], u[c, :M, :]], 0)
        disp_send[c] = disp_send[c] + jnp.sum(joined * step_coef, axis=0, keepdims=True)
        next_disp[c : c + 1, :] = disp_send[c]

    def table_copy(p):
        return remote(disp_send, row(table, me), ts_sem, tr_sem, p)

    others(lambda p: table_copy(p).start())
    pltpu.make_async_copy(disp_send, row(table, me), tr_sem).start()

    block(4)
    block(5)

    upper = jnp.where(iota((K, 256), 1) >= iota((K, 256), 0), aug[:, 0:256], 0.0)
    mix_u[...] = nn(upper[:, :K], change[:K])
    mix_z[...] = aug[:, 256:512]

    pltpu.make_async_copy(table, table, tr_sem).wait()
    for c in range(6):
        high, low = split(table[c])
        table_hi[c * n : (c + 1) * n, :] = high
        table_lo[c * n : (c + 1) * n, :] = low

    gram_blocks(lambda b, slot, p: gram_copy(b, slot, p).wait_send(), None)
    reducing(
        lambda slot, b: others(
            lambda p: remote(
                gram_sum.at[slot], gram_all.at[b], ga_send_sem, ga_sem, p
            ).wait_send()
        )
    )
    others(lambda p: load_copy(p).wait_send())
    others(lambda p: q_copy(p).wait_send())
    others(lambda p: table_copy(p).wait_send())


def finish_kernel(
    n, owner, target, table_hi, table_lo, mix_u, mix_z, u, z, v, w,
    u_out, z_out, wetted, u_buf, z_buf, sem,
):
    left_u = mix_u[:, :ROWS]
    left_z = mix_z[:, :K]
    for c in range(6):
        u_buf[c] = nn(left_u, jnp.concatenate([u[c, M:, :], w[c], u[c, :M, :]], 0))
        z_buf[c] = nn(left_z, jnp.concatenate([z[c, M:, :], v[c]], 0))
    u_copy = pltpu.make_async_copy(u_buf, u_out, sem.at[0])
    z_copy = pltpu.make_async_copy(z_buf, z_out, sem.at[1])
    u_copy.start()
    z_copy.start()

    faces = wetted.shape[1]
    chunk = min(FACE_CHUNK, faces)
    left = jnp.concatenate([table_hi[...], table_lo[...]], 1)

    def gather(i, carry):
        at = pl.ds(pl.multiple_of(i * chunk, chunk), chunk)
        at_owner = iota((n, chunk), 0) == owner[:, at]
        at_point = (iota((BLK, chunk), 0) == target[:, at]).astype(F32).astype(BF16)
        right = jnp.concatenate([at_point, at_point], 0)
        values = lax.dot_general(left, right, (((1,), (0,)), ((), ())), preferred_element_type=F32)
        rows = [
            jnp.sum(jnp.where(at_owner, values[c * n : (c + 1) * n], 0.0), axis=0, keepdims=True)
            for c in range(6)
        ]
        wetted[:, at] = jnp.concatenate(rows, 0)
        return carry

    lax.fori_loop(0, faces // chunk, gather, 0)
    u_copy.wait()
    z_copy.wait()


def on_device(n_g, n_r, force_rows, owners, target, rbf_blocks, displacement, u_basis, z_basis, v_new, w_new):
    n = n_g * n_r
    faces = force_rows.shape[1]
    reducers = min(n, GBLK)
    slots = -(-GBLK // reducers)
    owner = owners.reshape(1, faces)
    point = target.reshape(1, faces)
    u, z, v, w = (x.transpose(1, 0, 2) for x in (u_basis, z_basis, v_new, w_new))
    vmem = pl.BlockSpec(memory_space=pltpu.VMEM)
    table_hi, table_lo, mix_u, mix_z, next_disp = pl.pallas_call(
        functools.partial(exchange_kernel, n_g, n_r),
        out_shape=(
            jax.ShapeDtypeStruct((6 * n, BLK), BF16),
            jax.ShapeDtypeStruct((6 * n, BLK), BF16),
            jax.ShapeDtypeStruct((K, 256), F32),
            jax.ShapeDtypeStruct((K, 256), F32),
            jax.ShapeDtypeStruct((6, BLK), F32),
        ),
        in_specs=[vmem] * 9,
        out_specs=(vmem,) * 5,
        scratch_shapes=[
            pltpu.VMEM((GBLK, 8, 256), F32),
            pltpu.VMEM((slots, n, 8, 256), F32),
            pltpu.VMEM((slots, 8, 256), F32),
            pltpu.VMEM((GBLK, 8, 256), F32),
            pltpu.VMEM((6, n, BLK), F32),
            pltpu.VMEM((6, n, BLK), F32),
            pltpu.VMEM((1, 256), F32),
            pltpu.VMEM((n, 1, 256), F32),
            pltpu.VMEM((6, 1, BLK), F32),
            pltpu.VMEM((6, n, BLK), F32),
            pltpu.VMEM((K, 512), F32),
            pltpu.VMEM((ROWS, 256), F32),
            pltpu.SemaphoreType.DMA,
            pltpu.SemaphoreType.DMA((slots,)),
            pltpu.SemaphoreType.DMA,
            pltpu.SemaphoreType.DMA,
            pltpu.SemaphoreType.DMA,
            pltpu.SemaphoreType.DMA,
            pltpu.SemaphoreType.DMA,
            pltpu.SemaphoreType.DMA,
            pltpu.SemaphoreType.DMA,
            pltpu.SemaphoreType.DMA,
        ],
        compiler_params=pltpu.CompilerParams(collective_id=0, has_side_effects=True),
        name="exchange",
    )(force_rows, owner, point, rbf_blocks[0], displacement, u, z, v, w)
    u_out, z_out, wetted = pl.pallas_call(
        functools.partial(finish_kernel, n),
        out_shape=(
            jax.ShapeDtypeStruct((6, K, BLK), F32),
            jax.ShapeDtypeStruct((6, K, BLK), F32),
            jax.ShapeDtypeStruct((6, faces), F32),
        ),
        in_specs=[vmem] * 10,
        out_specs=(
            pl.BlockSpec(memory_space=pl.ANY),
            pl.BlockSpec(memory_space=pl.ANY),
            vmem,
        ),
        scratch_shapes=[
            pltpu.VMEM((6, K, BLK), F32),
            pltpu.VMEM((6, K, BLK), F32),
            pltpu.SemaphoreType.DMA((2,)),
        ],
        name="finish",
    )(owner, point, table_hi, table_lo, mix_u, mix_z, u, z, v, w)
    return u_out.transpose(1, 0, 2), z_out.transpose(1, 0, 2), next_disp, wetted


def solution(mesh):
    return jax.shard_map(
        functools.partial(on_device, mesh.shape["group"], mesh.shape["rows"]),
        mesh=mesh,
        in_specs=(
            P(None, AXES),
            P(AXES, None),
            P(AXES),
            P(AXES, None, None),
            P(None, AXES),
            P(None, None, AXES),
            P(None, None, AXES),
            P(None, None, AXES),
            P(None, None, AXES),
        ),
        out_specs=(P(None, None, AXES), P(None, None, AXES), P(None, AXES), P(None, AXES)),
        check_vma=False,
    )
```

time: 651 us -> 87.1 us (0.13); the launches traced: 640 us -> 87 us
  local copies, waits for them, and re-layouts: 324 us -> 0.61 us
  blocking collectives: 139 us -> 0 us
  other arithmetic: 125 us -> 0 us
  Pallas kernels: 0 us -> 85.7 us
  matrix products: 15.7 us -> 0 us
  between operations: 16.3 us -> 0.66 us
  starting transfers between devices: 11.2 us -> 0 us
  waiting for transfers between devices: 8.4 us -> 0 us
    gather x17 -> x0, local copies, waits for them, and re-layouts: 148 us -> none  [the longest x1 48.9 us: on_device(): slot_rank = jnp.arange(face_count, dtype=jnp.int32) - starts[dest_sorted]]
    psum x2 -> x0, blocking collectives: 139 us -> none  [on_device(): lax.psum((jnp.dot(z_flat, v_flat.T, precision=precise), jnp.dot(v_flat, v...]
    scatter x2 -> x0, local copies, waits for them, and re-layouts: 139 us -> none  [the longest x1 69.6 us: on_device(): jnp.zeros((7, n_devices * capacity), jnp.float32).at[:, slot_idx]]
    pallas_call x0 -> x2, Pallas kernels: none -> 85.7 us  [the longest x1 70.8 us: on_device(): pl.pallas_call(functools.partial(exchange_kernel, n_g, n_r), out_shape=(j...]
    another operation x19 -> x0, other arithmetic: 56.1 us -> none  [the longest x7 28.8 us: on_device(): chol_rest = jnp.linalg.cholesky(gram_rest)]
    scatter-add x1 -> x0, other arithmetic: 55.1 us -> none  [on_device(): jnp.zeros((6, points_dev), jnp.float32).at[:, spots_idx].add(arrived[:6])]
    all_to_all x4 -> x0, local copies, waits for them, and re-layouts: 11.4 us -> none  [the longest x3 7.13 us: on_device(): lax.all_to_all(outgoing, ('group', 'rows'), split_axis=1, concat_axis=1,...]
    all_to_all x2 -> x0, starting transfers between devices: 11.2 us -> none  [the longest x1 5.8 us: on_device(): lax.all_to_all(outgoing, ('group', 'rows'), split_axis=1, concat_axis=1,...]
  transfers between devices with their start and end apart: 3 -> 0, of which waited for: 1 -> 0; matrix products, arithmetic and copies ran while one was open for 41% -> 0% of each run, Pallas kernels for 0% -> 0%
where the time goes in v1:
time: 87.1 us; the launch traced here: 87 us
  Pallas kernels  85.7 us (98%)
    pallas_call x1, Pallas kernels, on_device(): pl.pallas_call(functools.partial(exchange_kernel, n_g, n_r), out_shape=(j...  70.8 us
    pallas_call x1, Pallas kernels, on_device(): pl.pallas_call(functools.partial(finish_kernel, n), out_shape=(jax.ShapeD...  14.9 us

profile of v1, /device:TPU:1, one launch (start us, length us, event | category | flops | bytes accessed | tf_op | source)
XLA Modules:
  0.0 87.0 jit_solution(3932494732984301192)
XLA Ops:
  0.6 70.8 %exchange.1 = (bf16[768,256]{1,0:T(8,128)(2,1)}, bf16[768,256]{1,0:T(8,128)(2,1)}, f32[192,256]{1,0:T(8,128)}, f32[192,256]{1,0:T(8,128)}, f32[6,256]{1,0:T(8,128)}) custom-call(f32[6,8192]{1,0:T(8,128)} %force.1, s32[1,8192]{1,0:T(1,128)} %bitcast.18, s32[1,8192]{1,0:T(1,128)} %bitcast.20, f32[256,256]{1,0:T(8,128)} %bitcast.17, f32[6,256]{1,0:T(8,128)} %disp.1, ...), custom_call_target="tpu_custom_call" | custom-call | tf_op jit(solution)/shard_map/exchange/pallas_call | solution.py:352
  71.4 0.0 copy-start
  71.4 14.9 %finish.1 = (f32[6,192,256]{2,1,0:T(8,128)}, f32[6,192,256]{2,1,0:T(8,128)}, f32[6,8192]{1,0:T(8,128)}) custom-call(s32[1,8192]{1,0:T(1,128)} %bitcast.19, s32[1,8192]{1,0:T(1,128)} %bitcast.21, bf16[768,256]{1,0:T(8,128)(2,1)} %get-tuple-element.12.table_hi, bf16[768,256]{1,0:T(8,128)(2,1)} %get-tuple-element.13.table_lo, ...), custom_call_target="tpu_custom_call" | custom-call | tf_op jit(solution)/shard_map/finish/pallas_call | solution.py:390
  86.3 0.0 copy-done
  86.4 0.6 copy.14
Async XLA Ops:
  71.4 14.9 %copy-start = (f32[6,256]{1,0:T(8,128)S(1)}, f32[6,256]{1,0:T(8,128)}, u32[]{:S(2)}) copy-start(f32[6,256]{1,0:T(8,128)} %get-tuple-element.26) | copy-start | bytes 18436

commit v2 on v1

v2 whole, which is shorter than its diff:
```python
import functools

import jax
import jax.numpy as jnp
from jax import lax
from jax.experimental import pallas as pl
from jax.experimental.pallas import tpu as pltpu
from jax.sharding import PartitionSpec as P

BLK = 256
K = 192
M = 32
KEEP = K - M
NB = 32
ROWS = K + M
GBLK = ROWS // 8
FACE_CHUNK = 2048
GATHER_CHUNK = 1024
UNROLL = 8

MESH = pl.DeviceIdType.MESH
F32 = jnp.float32
BF16 = jnp.bfloat16
AXES = ("group", "rows")


def iota(shape, dim):
    return lax.broadcasted_iota(jnp.int32, shape, dim)


def dot(a, b, dims):
    return lax.dot_general(
        a, b, (dims, ((), ())), precision=lax.Precision.HIGHEST, preferred_element_type=F32
    )


def nn(a, b):
    return dot(a, b, ((1,), (0,)))


def nt(a, b):
    return dot(a, b, ((1,), (1,)))


def tn(a, b):
    return dot(a, b, ((0,), (0,)))


def split(x):
    high = x.astype(BF16)
    return high, (x - high.astype(F32)).astype(BF16)


def eliminate(tiles, first):
    rows = iota((NB, 128), 0)
    tiles = list(tiles)
    base = first // 128
    for j in range(0, NB, 4):
        lane = first % 128 + j
        pivot_tile = tiles[base]
        c = [jnp.broadcast_to(pivot_tile[:, lane + i : lane + i + 1], (NB, 128)) for i in range(4)]
        a = {
            (i, k): jnp.broadcast_to(c[k][j + i : j + i + 1, :], (NB, 128))
            for i in range(4)
            for k in range(i, 4)
        }
        p0 = 1.0 / a[0, 0]
        l1, l2, l3 = a[0, 1] * p0, a[0, 2] * p0, a[0, 3] * p0
        b11, b12, b13 = a[1, 1] - l1 * a[0, 1], a[1, 2] - l1 * a[0, 2], a[1, 3] - l1 * a[0, 3]
        b22, b23, b33 = a[2, 2] - l2 * a[0, 2], a[2, 3] - l2 * a[0, 3], a[3, 3] - l3 * a[0, 3]
        p1 = 1.0 / b11
        l21, l31 = b12 * p1, b13 * p1
        b22, b23, b33 = b22 - l21 * b12, b23 - l21 * b13, b33 - l31 * b13
        p2 = 1.0 / b22
        l32 = b23 * p2
        p3 = 1.0 / (b33 - l32 * b23)
        m0 = jnp.where(rows > j, c[0] * p0, 0.0)
        m1 = jnp.where(rows > j + 1, (c[1] - m0 * a[0, 1]) * p1, 0.0)
        m2 = jnp.where(rows > j + 2, (c[2] - m0 * a[0, 2] - m1 * b12) * p2, 0.0)
        m3 = jnp.where(rows > j + 3, (c[3] - m0 * a[0, 3] - m1 * b13 - m2 * b23) * p3, 0.0)
        m2 = m2 - m3 * l32
        m1 = m1 - m2 * l21 - m3 * l31
        m0 = m0 - m1 * l1 - m2 * l2 - m3 * l3
        for t, tile in enumerate(tiles):
            r = [tile[j + i : j + i + 1, :] for i in range(4)]
            tiles[t] = tile - (m0 * r[0] + m1 * r[1]) - (m2 * r[2] + m3 * r[3])
    own = iota((NB, 128), 1) == first % 128 + rows
    pivots = jnp.sum(jnp.where(own, tiles[base], 0.0), axis=1, keepdims=True)
    scale = lax.rsqrt(pivots)
    return [tile * scale for tile in tiles]
def exchange_kernel(
    n_g, n_r,
    force, owner, target, rbf_any, disp_any, u_any, z_any, v_any, w_any,
    table_hi, table_lo, mix_u, mix_z, next_disp,
    rbf, disp, u, z, v, w,
    gram_send, gram_recv, gram_sum, gram_all,
    load_pair, load_own, pair_recv, load_recv, q_send, q_recv, disp_send, table_own, table_pair,
    aug, coef_scr,
    in_sem, gs_sem, gr_sem, ga_send_sem, ga_sem, ps_sem, pr_sem, ls_sem, lr_sem,
    qs_sem, qr_sem, ts_sem, tr_sem, fs_sem, fr_sem,
):
    n = n_g * n_r
    half = n // 2
    me = lax.axis_index("group") * n_r + lax.axis_index("rows")
    chip, core = me // 2, lax.rem(me, 2)
    reducers = min(n, GBLK)
    stride = n // 32 if n >= 32 else 1
    slots = -(-GBLK // reducers)
    dof_total = 6 * BLK * n

    def device(p):
        return (p // n_r, lax.rem(p, n_r))

    def others(body, unroll=1):
        def step(k, carry):
            body(lax.rem(me + k, n))
            return carry

        lax.fori_loop(1, n, step, 0, unroll=unroll)

    def other_chips(body, unroll=1):
        def step(k, carry):
            body(lax.rem(chip + k, half))
            return carry

        lax.fori_loop(1, half, step, 0, unroll=unroll)

    def remote(src, dst, send, recv, p):
        return pltpu.make_async_remote_copy(
            src_ref=src, dst_ref=dst, send_sem=send, recv_sem=recv,
            device_id=device(p), device_id_type=MESH,
        )

    loads = [
        pltpu.make_async_copy(src, dst, in_sem.at[i])
        for i, (src, dst) in enumerate(
            ((z_any, z), (v_any, v), (rbf_any, rbf), (disp_any, disp), (u_any, u), (w_any, w))
        )
    ]
    for copy in loads:
        copy.start()
    barrier = pltpu.get_barrier_semaphore()
    others(
        lambda p: pl.semaphore_signal(barrier, inc=1, device_id=device(p), device_id_type=MESH),
        UNROLL,
    )

    loads[0].wait()
    loads[1].wait()
    gram = jnp.zeros((ROWS, ROWS), F32)
    for c in range(6):
        joined = jnp.concatenate([z[c, M:, :], v[c], z[c, :M, :]], 0)
        gram = gram + nt(joined, joined)
    gram = gram * (1.0 / dof_total)
    gram = jnp.concatenate([gram, jnp.zeros((ROWS, 256 - ROWS), F32)], 1)
    gram_send[...] = gram.reshape(GBLK, 8, 256)

    faces = force.shape[1]
    chunk = min(FACE_CHUNK, faces)

    def scatter_to(load, parity):
        def scatter(i, carry):
            at = pl.ds(pl.multiple_of(i * chunk, chunk), chunk)
            named = iota((half, chunk), 0) * 2 + parity
            at_owner = (named == owner[:, at]).astype(F32).astype(BF16)
            at_point = (iota((BLK, chunk), 0) == target[:, at]).astype(F32).astype(BF16)
            high, low = split(force[:, at])
            left = jnp.concatenate(
                [
                    jnp.concatenate([at_owner * high[c : c + 1], at_owner * low[c : c + 1]], 1)
                    for c in range(6)
                ],
                0,
            )
            right = jnp.concatenate([at_point, at_point], 1)
            add = lax.dot_general(
                left, right, (((1,), (1,)), ((), ())), preferred_element_type=F32
            )
            load[...] += add.reshape(6, half, BLK)
            return carry

        load[...] = jnp.zeros_like(load)
        lax.fori_loop(0, faces // chunk, scatter, 0)

    scatter_to(load_pair, 1 - core)

    pl.semaphore_wait(barrier, n - 1)

    def gram_blocks(away, here):
        def step(b, carry):
            slot, p = b // reducers, lax.rem(b, reducers) * stride

            @pl.when(p != me)
            def _():
                away(b, slot, p)

            if here is not None:

                @pl.when(p == me)
                def _():
                    here(b, slot)

            return carry

        lax.fori_loop(0, GBLK, step, 0)

    def gram_copy(b, slot, p):
        return remote(gram_send.at[b], gram_recv.at[slot, me], gs_sem, gr_sem.at[slot], p)

    gram_blocks(
        lambda b, slot, p: gram_copy(b, slot, p).start(),
        lambda b, slot: pltpu.make_async_copy(
            gram_send.at[b], gram_recv.at[slot, me], gr_sem.at[slot]
        ).start(),
    )
    partner = 2 * chip + 1 - core
    pair_copy = remote(load_pair, pair_recv, ps_sem, pr_sem, partner)
    pair_copy.start()

    scatter_to(load_own, core)

    pair_copy.wait_recv()
    load_own[...] += pair_recv[...]

    def row(ref, p):
        return ref.at[:, pl.ds(p, 1), :]

    def load_copy(p):
        return remote(row(load_own, p), row(load_recv, chip), ls_sem, lr_sem, 2 * p + core)

    other_chips(lambda p: load_copy(p).start(), UNROLL)
    pltpu.make_async_copy(row(load_own, chip), row(load_recv, chip), lr_sem).start()

    def reducing(body):
        for slot in range(slots):
            b = slot * reducers + me // stride

            @pl.when((lax.rem(me, stride) == 0) & (me // stride < reducers) & (b < GBLK))
            def _():
                body(slot, b)

    def reduce_gram(slot, b):
        pltpu.make_async_copy(gram_recv.at[slot], gram_recv.at[slot], gr_sem.at[slot]).wait()
        gram_sum[slot] = jnp.sum(gram_recv[slot], axis=0)

    reducing(reduce_gram)

    def share_copy(slot, b, p):
        return remote(gram_sum.at[slot], gram_all.at[b], ga_send_sem, ga_sem, p)

    def share_gram(slot, b):
        others(lambda p: share_copy(slot, b, p).start(), UNROLL)
        pltpu.make_async_copy(gram_sum.at[slot], gram_all.at[b], ga_sem).start()

    reducing(share_gram)
    for copy in loads[2:]:
        copy.wait()

    pltpu.make_async_copy(load_recv, load_recv, lr_sem).wait()
    point_load = jnp.concatenate(
        [jnp.sum(load_recv[c], axis=0, keepdims=True) for c in range(6)], 0
    )
    response = nn(point_load, rbf[...])
    residual = response - disp[...]
    disp_send[...] = response.reshape(6, 1, BLK)
    weighted = jnp.zeros((K, BLK), F32)
    for c in range(6):
        kept = jnp.concatenate([z[c, M:, :], v[c]], 0)
        weighted = weighted + kept * residual[c : c + 1]
    q_column = jnp.sum(weighted, axis=1, keepdims=True) * (1.0 / dof_total)
    diagonal = iota((K, 256), 0) == iota((K, 256), 1)
    q_send[...] = jnp.sum(jnp.where(diagonal, q_column, 0.0), axis=0, keepdims=True)

    def q_copy(p):
        return remote(q_send, q_recv.at[me], qs_sem, qr_sem, p)

    others(lambda p: q_copy(p).start(), UNROLL)
    pltpu.make_async_copy(q_send, q_recv.at[me], qr_sem).start()

    pltpu.make_async_copy(gram_all, gram_all, ga_sem).wait()
    total = gram_all[...].reshape(ROWS, 256)

    lane32 = iota((NB, 128), 1)
    row32 = iota((NB, 128), 0)
    middle = (lane32 >= 32) & (lane32 < 64)
    start = jnp.where(middle, total[KEEP:K, 128:], jnp.where(lane32 - 64 == row32, 1.0, 0.0))
    factor = pltpu.roll(eliminate([start], 32)[0], 96, 1)
    factor = jnp.where(middle, factor, 0.0)
    inverse = tn(factor, factor)
    scaled = nn(total[:, 128:], inverse)

    lanes = iota((ROWS, 256), 1)
    index = iota((ROWS, 256), 0)
    new_lane = (lanes >= KEEP) & (lanes < K)
    new_row = (index >= KEEP) & (index < K)
    scaled = jnp.concatenate([jnp.zeros((ROWS, 128), F32), scaled], 1)
    inverse_rows = jnp.concatenate(
        [jnp.zeros((KEEP, 128), F32), inverse[32:64], jnp.zeros((M, 128), F32)], 0
    )
    inverse_full = jnp.concatenate([jnp.zeros((ROWS, 128), F32), inverse_rows], 1)
    unit = jnp.where(lanes == index, 1.0, 0.0)
    matrix = jnp.where(new_lane, jnp.where(new_row, inverse_full, scaled), total)
    matrix = jnp.where(lanes < K, matrix, 0.0)
    extra = jnp.where(new_lane, inverse_full, unit)
    aug[:, 0:256] = matrix[:K]
    aug[:, 256:512] = extra[:K]
    coef_scr[...] = jnp.where(
        new_lane,
        jnp.where(new_row, inverse_full, -scaled),
        jnp.where(lanes < KEEP, unit, 0.0),
    )
    change = jnp.where(lanes == index, 1.0, jnp.where(new_row & (lanes < ROWS), -total, 0.0))
    change = jnp.where(new_row & new_lane, unit, change)[:K]

    def tile(t):
        return slice(t * 128, t * 128 + 128)

    def block(b):
        r0, after = b * NB, b * NB + NB
        rows = slice(r0, after)
        active = [0, 1, 2] if after <= 128 else [1, 2, 3]
        done = eliminate([aug[rows, tile(t)] for t in active], r0 - 128 * active[0])
        lane = iota((NB, 128), 1)
        for i, t in enumerate(active):
            if t < 2:
                done[i] = jnp.where(lane + t * 128 < r0, 0.0, done[i])
            aug[rows, tile(t)] = done[i]
        if after < K:
            first = after // 128
            left = [done[i] for i, t in enumerate(active) if first <= t < 2]
            changed = [(i, t) for i, t in enumerate(active) if t >= first]
            update = tn(
                jnp.concatenate(left, 1), jnp.concatenate([done[i] for i, _ in changed], 1)
            )
            part = update[after - 128 * first : K - 128 * first]
            for s, (_, t) in enumerate(changed):
                aug[after:K, tile(t)] = aug[after:K, tile(t)] - part[:, tile(s)]

    block(0)
    block(1)

    pltpu.make_async_copy(q_recv, q_recv, qr_sem).wait()
    q_row = jnp.sum(q_recv[...], axis=0)
    step_coef = jnp.sum(coef_scr[...] * q_row, axis=1, keepdims=True)
    for c in range(6):
        joined = jnp.concatenate([u[c, M:, :], w[c], u[c, :M, :]], 0)
        disp_send[c] = disp_send[c] + jnp.sum(joined * step_coef, axis=0, keepdims=True)
        next_disp[c : c + 1, :] = disp_send[c]

    def table_copy(p):
        return remote(disp_send, row(table_own, chip), ts_sem, tr_sem, 2 * p + core)

    other_chips(lambda p: table_copy(p).start(), UNROLL)
    pltpu.make_async_copy(disp_send, row(table_own, chip), tr_sem).start()

    for b in range(2, K // NB):
        block(b)

    upper = jnp.where(iota((K, 256), 1) >= iota((K, 256), 0), aug[:, 0:256], 0.0)
    mix_u[...] = nn(upper[:, :K], change)
    mix_z[...] = aug[:, 256:512]

    gram_blocks(lambda b, slot, p: gram_copy(b, slot, p).wait_send(), None)
    reducing(lambda slot, b: others(lambda p: share_copy(slot, b, p).wait_send()))
    pair_copy.wait_send()
    other_chips(lambda p: load_copy(p).wait_send())
    others(lambda p: q_copy(p).wait_send())

    pltpu.make_async_copy(table_own, table_own, tr_sem).wait()
    forward = remote(table_own, table_pair, fs_sem, fr_sem, partner)
    forward.start()

    def put(table, parity):
        for c in range(6):
            high, low = split(table[c])
            at = pl.ds(pl.multiple_of(c * n + parity * half, half), half)
            table_hi[at, :] = high
            table_lo[at, :] = low

    put(table_own, core)
    other_chips(lambda p: table_copy(p).wait_send())
    forward.wait_recv()
    put(table_pair, 1 - core)
    forward.wait_send()


def finish_kernel(
    n, owner, target, table_hi, table_lo, mix_u, mix_z, u_any, z_any, v_any, w_any,
    u_out, z_out, wetted, u, z, v, w, u_buf, z_buf, in_sem, sem,
):
    loads = [
        pltpu.make_async_copy(src, dst, in_sem.at[i])
        for i, (src, dst) in enumerate(((u_any, u), (z_any, z), (v_any, v), (w_any, w)))
    ]
    for copy in loads:
        copy.start()
    half = n // 2
    faces = wetted.shape[1]
    chunk = min(GATHER_CHUNK, faces // 2)
    left = jnp.concatenate([table_hi[...], table_lo[...]], 1)

    def gather(i, carry):
        at = pl.ds(pl.multiple_of(i * chunk, chunk), chunk)
        name = owner[:, at]
        place = (name & 1) * half + (name >> 1)
        at_owner = iota((n, chunk), 0) == place
        at_point = (iota((BLK, chunk), 0) == target[:, at]).astype(F32).astype(BF16)
        right = jnp.concatenate([at_point, at_point], 0)
        values = lax.dot_general(left, right, (((1,), (0,)), ((), ())), preferred_element_type=F32)
        rows = [
            jnp.sum(jnp.where(at_owner, values[c * n : (c + 1) * n], 0.0), axis=0, keepdims=True)
            for c in range(6)
        ]
        wetted[:, at] = jnp.concatenate(rows, 0)
        return carry

    steps = faces // chunk
    lax.fori_loop(0, steps // 2, gather, 0)

    for copy in loads:
        copy.wait()
    left_u = mix_u[:, :ROWS]
    left_z = mix_z[:, :K]
    for c in range(6):
        u_buf[c] = nn(left_u, jnp.concatenate([u[c, M:, :], w[c], u[c, :M, :]], 0))
        z_buf[c] = nn(left_z, jnp.concatenate([z[c, M:, :], v[c]], 0))
    u_copy = pltpu.make_async_copy(u_buf, u_out, sem.at[0])
    z_copy = pltpu.make_async_copy(z_buf, z_out, sem.at[1])
    u_copy.start()
    z_copy.start()

    lax.fori_loop(steps // 2, steps, gather, 0)
    u_copy.wait()
    z_copy.wait()


def on_device(n_g, n_r, force_rows, owners, target, rbf_blocks, displacement, u_basis, z_basis, v_new, w_new):
    n = n_g * n_r
    half = n // 2
    faces = force_rows.shape[1]
    reducers = min(n, GBLK)
    slots = -(-GBLK // reducers)
    owner = owners.reshape(1, faces)
    point = target.reshape(1, faces)
    u, z, v, w = (x.transpose(1, 0, 2) for x in (u_basis, z_basis, v_new, w_new))
    vmem = pl.BlockSpec(memory_space=pltpu.VMEM)
    away = pl.BlockSpec(memory_space=pl.ANY)
    dma = pltpu.SemaphoreType.DMA
    table_hi, table_lo, mix_u, mix_z, next_disp = pl.pallas_call(
        functools.partial(exchange_kernel, n_g, n_r),
        out_shape=(
            jax.ShapeDtypeStruct((6 * n, BLK), BF16),
            jax.ShapeDtypeStruct((6 * n, BLK), BF16),
            jax.ShapeDtypeStruct((K, 256), F32),
            jax.ShapeDtypeStruct((K, 256), F32),
            jax.ShapeDtypeStruct((6, BLK), F32),
        ),
        in_specs=[vmem] * 3 + [away] * 6,
        out_specs=(vmem,) * 5,
        scratch_shapes=[
            pltpu.VMEM((BLK, BLK), F32),
            pltpu.VMEM((6, BLK), F32),
            pltpu.VMEM((6, K, BLK), F32),
            pltpu.VMEM((6, K, BLK), F32),
            pltpu.VMEM((6, M, BLK), F32),
            pltpu.VMEM((6, M, BLK), F32),
            pltpu.VMEM((GBLK, 8, 256), F32),
            pltpu.VMEM((slots, n, 8, 256), F32),
            pltpu.VMEM((slots, 8, 256), F32),
            pltpu.VMEM((GBLK, 8, 256), F32),
            pltpu.VMEM((6, half, BLK), F32),
            pltpu.VMEM((6, half, BLK), F32),
            pltpu.VMEM((6, half, BLK), F32),
            pltpu.VMEM((6, half, BLK), F32),
            pltpu.VMEM((1, 256), F32),
            pltpu.VMEM((n, 1, 256), F32),
            pltpu.VMEM((6, 1, BLK), F32),
            pltpu.VMEM((6, half, BLK), F32),
            pltpu.VMEM((6, half, BLK), F32),
            pltpu.VMEM((K, 512), F32),
            pltpu.VMEM((ROWS, 256), F32),
            dma((6,)),
            dma,
            dma((slots,)),
        ]
        + [dma] * 12,
        compiler_params=pltpu.CompilerParams(collective_id=0, has_side_effects=True),
        name="exchange",
    )(force_rows, owner, point, rbf_blocks[0], displacement, u, z, v, w)
    u_out, z_out, wetted = pl.pallas_call(
        functools.partial(finish_kernel, n),
        out_shape=(
            jax.ShapeDtypeStruct((6, K, BLK), F32),
            jax.ShapeDtypeStruct((6, K, BLK), F32),
            jax.ShapeDtypeStruct((6, faces), F32),
        ),
        in_specs=[vmem] * 6 + [away] * 4,
        out_specs=(away, away, vmem),
        scratch_shapes=[
            pltpu.VMEM((6, K, BLK), F32),
            pltpu.VMEM((6, K, BLK), F32),
            pltpu.VMEM((6, M, BLK), F32),
            pltpu.VMEM((6, M, BLK), F32),
            pltpu.VMEM((6, K, BLK), F32),
            pltpu.VMEM((6, K, BLK), F32),
            dma((4,)),
            dma((2,)),
        ],
        name="finish",
    )(owner, point, table_hi, table_lo, mix_u, mix_z, u, z, v, w)
    return u_out.transpose(1, 0, 2), z_out.transpose(1, 0, 2), next_disp, wetted


def solution(mesh):
    return jax.shard_map(
        functools.partial(on_device, mesh.shape["group"], mesh.shape["rows"]),
        mesh=mesh,
        in_specs=(
            P(None, AXES),
            P(AXES, None),
            P(AXES),
            P(AXES, None, None),
            P(None, AXES),
            P(None, None, AXES),
            P(None, None, AXES),
            P(None, None, AXES),
            P(None, None, AXES),
        ),
        out_specs=(P(None, None, AXES), P(None, None, AXES), P(None, AXES), P(None, AXES)),
        check_vma=False,
    )
```

time: 87.1 us -> 68.8 us (0.79)
  Pallas kernels: 85.7 us -> 67.3 us
    pallas_call x1, Pallas kernels: 70.8 us -> 54.5 us  [on_device(): pl.pallas_call(functools.partial(exchange_kernel, n_g, n_r), out_shape=(j...]
    pallas_call x1, Pallas kernels: 14.9 us -> 12.8 us  [on_device(): pl.pallas_call(functools.partial(finish_kernel, n), out_shape=(jax.ShapeD...]
where the time goes in v2:
time: 68.8 us; the launch traced here: 68.6 us
  Pallas kernels  67.3 us (98%)
    pallas_call x1, Pallas kernels, on_device(): pl.pallas_call(functools.partial(exchange_kernel, n_g, n_r), out_shape=(j...  54.5 us
    pallas_call x1, Pallas kernels, on_device(): pl.pallas_call(functools.partial(finish_kernel, n), out_shape=(jax.ShapeD...  12.8 us

profile of v2, /device:TPU:1, one launch (start us, length us, event | category | flops | bytes accessed | tf_op | source)
XLA Modules:
  0.0 68.6 jit_solution(17140574229006660174)
XLA Ops:
  0.6 54.5 %exchange.1 = (bf16[768,256]{1,0:T(8,128)(2,1)}, bf16[768,256]{1,0:T(8,128)(2,1)}, f32[192,256]{1,0:T(8,128)}, f32[192,256]{1,0:T(8,128)}, f32[6,256]{1,0:T(8,128)}) custom-call(f32[6,8192]{1,0:T(8,128)} %force.1, s32[1,8192]{1,0:T(1,128)} %bitcast.18, s32[1,8192]{1,0:T(1,128)} %bitcast.20, f32[256,256]{1,0:T(8,128)} %bitcast.17, f32[6,256]{1,0:T(8,128)} %disp_any.1, ...), custom_call_target="tpu_custom_call" | custom-call | tf_op jit(solution)/shard_map/exchange/pallas_call | solution.py:449
  55.1 0.0 copy-start
  55.2 12.8 %finish.1 = (f32[6,192,256]{2,1,0:T(8,128)}, f32[6,192,256]{2,1,0:T(8,128)}, f32[6,8192]{1,0:T(8,128)}) custom-call(s32[1,8192]{1,0:T(1,128)} %bitcast.19, s32[1,8192]{1,0:T(1,128)} %bitcast.21, bf16[768,256]{1,0:T(8,128)(2,1)} %get-tuple-element.12.table_hi, bf16[768,256]{1,0:T(8,128)(2,1)} %get-tuple-element.13.table_lo, ...), custom_call_target="tpu_custom_call" | custom-call | tf_op jit(solution)/shard_map/finish/pallas_call | solution.py:490
  68.0 0.0 copy-done
  68.0 0.6 copy.14
Async XLA Ops:
  55.1 12.9 %copy-start = (f32[6,256]{1,0:T(8,128)S(1)}, f32[6,256]{1,0:T(8,128)}, u32[]{:S(2)}) copy-start(f32[6,256]{1,0:T(8,128)} %get-tuple-element.26) | copy-start | bytes 18436

commit v3 on v2

--- a/solution.py
+++ b/solution.py
@@ -13,9 +13,9 @@
 KEEP = K - M
 NB = 32
 ROWS = K + M
-GBLK = ROWS // 8
+SHARES = ROWS // 2
 FACE_CHUNK = 2048
-GATHER_CHUNK = 1024
+GATHER_CHUNK = 2048
 UNROLL = 8
 
 MESH = pl.DeviceIdType.MESH
@@ -103,9 +103,6 @@
     half = n // 2
     me = lax.axis_index("group") * n_r + lax.axis_index("rows")
     chip, core = me // 2, lax.rem(me, 2)
-    reducers = min(n, GBLK)
-    stride = n // 32 if n >= 32 else 1
-    slots = -(-GBLK // reducers)
     dof_total = 6 * BLK * n
 
     def device(p):
@@ -153,7 +150,7 @@
         gram = gram + nt(joined, joined)
     gram = gram * (1.0 / dof_total)
     gram = jnp.concatenate([gram, jnp.zeros((ROWS, 256 - ROWS), F32)], 1)
-    gram_send[...] = gram.reshape(GBLK, 8, 256)
+    gram_send[...] = gram.reshape(2, SHARES, 256)
 
     faces = force.shape[1]
     chunk = min(FACE_CHUNK, faces)
@@ -186,33 +183,26 @@
 
     pl.semaphore_wait(barrier, n - 1)
 
-    def gram_blocks(away, here):
-        def step(b, carry):
-            slot, p = b // reducers, lax.rem(b, reducers) * stride
-
-            @pl.when(p != me)
+    def row(ref, p):
+        return ref.at[:, pl.ds(p, 1), :]
+
+    def gram_copy(p):
+        return remote(row(gram_send, p), row(gram_recv, me), gs_sem, gr_sem, p)
+
+    def to_shares(body, unroll=1):
+        def guarded(p):
+            @pl.when(p < SHARES)
             def _():
-                away(b, slot, p)
-
-            if here is not None:
-
-                @pl.when(p == me)
-                def _():
-                    here(b, slot)
-
-            return carry
-
-        lax.fori_loop(0, GBLK, step, 0)
-
-    def gram_copy(b, slot, p):
-        return remote(gram_send.at[b], gram_recv.at[slot, me], gs_sem, gr_sem.at[slot], p)
-
-    gram_blocks(
-        lambda b, slot, p: gram_copy(b, slot, p).start(),
-        lambda b, slot: pltpu.make_async_copy(
-            gram_send.at[b], gram_recv.at[slot, me], gr_sem.at[slot]
-        ).start(),
-    )
+                body(p)
+
+        others(guarded, unroll)
+
+    to_shares(lambda p: gram_copy(p).start(), UNROLL)
+
+    @pl.when(me < SHARES)
+    def _():
+        pltpu.make_async_copy(row(gram_send, me), row(gram_recv, me), gr_sem).start()
+
     partner = 2 * chip + 1 - core
     pair_copy = remote(load_pair, pair_recv, ps_sem, pr_sem, partner)
     pair_copy.start()
@@ -222,37 +212,23 @@
     pair_copy.wait_recv()
     load_own[...] += pair_recv[...]
 
-    def row(ref, p):
-        return ref.at[:, pl.ds(p, 1), :]
-
     def load_copy(p):
         return remote(row(load_own, p), row(load_recv, chip), ls_sem, lr_sem, 2 * p + core)
 
     other_chips(lambda p: load_copy(p).start(), UNROLL)
     pltpu.make_async_copy(row(load_own, chip), row(load_recv, chip), lr_sem).start()
 
-    def reducing(body):
-        for slot in range(slots):
-            b = slot * reducers + me // stride
-
-            @pl.when((lax.rem(me, stride) == 0) & (me // stride < reducers) & (b < GBLK))
-            def _():
-                body(slot, b)
-
-    def reduce_gram(slot, b):
-        pltpu.make_async_copy(gram_recv.at[slot], gram_recv.at[slot], gr_sem.at[slot]).wait()
-        gram_sum[slot] = jnp.sum(gram_recv[slot], axis=0)
-
-    reducing(reduce_gram)
-
-    def share_copy(slot, b, p):
-        return remote(gram_sum.at[slot], gram_all.at[b], ga_send_sem, ga_sem, p)
-
-    def share_gram(slot, b):
-        others(lambda p: share_copy(slot, b, p).start(), UNROLL)
-        pltpu.make_async_copy(gram_sum.at[slot], gram_all.at[b], ga_sem).start()
-
-    reducing(share_gram)
+    def share_copy(p):
+        return remote(gram_sum, row(gram_all, me), ga_send_sem, ga_sem, p)
+
+    @pl.when(me < SHARES)
+    def _():
+        pltpu.make_async_copy(gram_recv, gram_recv, gr_sem).wait()
+        for i in range(2):
+            gram_sum[i] = jnp.sum(gram_recv[i], axis=0, keepdims=True)
+        others(lambda p: share_copy(p).start(), UNROLL)
+        pltpu.make_async_copy(gram_sum, row(gram_all, me), ga_sem).start()
+
     for copy in loads[2:]:
         copy.wait()
 
@@ -337,7 +313,6 @@
                 aug[after:K, tile(t)] = aug[after:K, tile(t)] - part[:, tile(s)]
 
     block(0)
-    block(1)
 
     pltpu.make_async_copy(q_recv, q_recv, qr_sem).wait()
     q_row = jnp.sum(q_recv[...], axis=0)
@@ -353,15 +328,19 @@
     other_chips(lambda p: table_copy(p).start(), UNROLL)
     pltpu.make_async_copy(disp_send, row(table_own, chip), tr_sem).start()
 
-    for b in range(2, K // NB):
+    for b in range(1, K // NB):
         block(b)
 
     upper = jnp.where(iota((K, 256), 1) >= iota((K, 256), 0), aug[:, 0:256], 0.0)
     mix_u[...] = nn(upper[:, :K], change)
     mix_z[...] = aug[:, 256:512]
 
-    gram_blocks(lambda b, slot, p: gram_copy(b, slot, p).wait_send(), None)
-    reducing(lambda slot, b: others(lambda p: share_copy(slot, b, p).wait_send()))
+    to_shares(lambda p: gram_copy(p).wait_send())
+
+    @pl.when(me < SHARES)
+    def _():
+        others(lambda p: share_copy(p).wait_send())
+
     pair_copy.wait_send()
     other_chips(lambda p: load_copy(p).wait_send())
     others(lambda p: q_copy(p).wait_send())
@@ -385,8 +364,8 @@
 
 
 def finish_kernel(
-    n, owner, target, table_hi, table_lo, mix_u, mix_z, u_any, z_any, v_any, w_any,
-    u_out, z_out, wetted, u, z, v, w, u_buf, z_buf, in_sem, sem,
+    n, owner, target, table_hi, table_lo, mix_u, mix_z, disp_in, u_any, z_any, v_any, w_any,
+    u_out, z_out, disp_out, wetted, u, z, v, w, u_buf, z_buf, in_sem, sem,
 ):
     loads = [
         pltpu.make_async_copy(src, dst, in_sem.at[i])
@@ -394,6 +373,7 @@
     ]
     for copy in loads:
         copy.start()
+    disp_out[...] = disp_in[...]
     half = n // 2
     faces = wetted.shape[1]
     chunk = min(GATHER_CHUNK, faces // 2)
@@ -438,8 +418,6 @@
     n = n_g * n_r
     half = n // 2
     faces = force_rows.shape[1]
-    reducers = min(n, GBLK)
-    slots = -(-GBLK // reducers)
     owner = owners.reshape(1, faces)
     point = target.reshape(1, faces)
     u, z, v, w = (x.transpose(1, 0, 2) for x in (u_basis, z_basis, v_new, w_new))
@@ -464,10 +442,10 @@
             pltpu.VMEM((6, K, BLK), F32),
             pltpu.VMEM((6, M, BLK), F32),
             pltpu.VMEM((6, M, BLK), F32),
-            pltpu.VMEM((GBLK, 8, 256), F32),
-            pltpu.VMEM((slots, n, 8, 256), F32),
-            pltpu.VMEM((slots, 8, 256), F32),
-            pltpu.VMEM((GBLK, 8, 256), F32),
+            pltpu.VMEM((2, SHARES, 256), F32),
+            pltpu.VMEM((2, n, 256), F32),
+            pltpu.VMEM((2, 1, 256), F32),
+            pltpu.VMEM((2, SHARES, 256), F32),
             pltpu.VMEM((6, half, BLK), F32),
             pltpu.VMEM((6, half, BLK), F32),
             pltpu.VMEM((6, half, BLK), F32),
@@ -480,22 +458,21 @@
             pltpu.VMEM((K, 512), F32),
             pltpu.VMEM((ROWS, 256), F32),
             dma((6,)),
-            dma,
-            dma((slots,)),
         ]
-        + [dma] * 12,
+        + [dma] * 14,
         compiler_params=pltpu.CompilerParams(collective_id=0, has_side_effects=True),
         name="exchange",
     )(force_rows, owner, point, rbf_blocks[0], displacement, u, z, v, w)
-    u_out, z_out, wetted = pl.pallas_call(
+    u_out, z_out, next_disp, wetted = pl.pallas_call(
         functools.partial(finish_kernel, n),
         out_shape=(
             jax.ShapeDtypeStruct((6, K, BLK), F32),
             jax.ShapeDtypeStruct((6, K, BLK), F32),
+            jax.ShapeDtypeStruct((6, BLK), F32),
             jax.ShapeDtypeStruct((6, faces), F32),
         ),
-        in_specs=[vmem] * 6 + [away] * 4,
-        out_specs=(away, away, vmem),
+        in_specs=[vmem] * 7 + [away] * 4,
+        out_specs=(away, away, vmem, vmem),
         scratch_shapes=[
             pltpu.VMEM((6, K, BLK), F32),
             pltpu.VMEM((6, K, BLK), F32),
@@ -507,7 +484,7 @@
             dma((2,)),
         ],
         name="finish",
-    )(owner, point, table_hi, table_lo, mix_u, mix_z, u, z, v, w)
+    )(owner, point, table_hi, table_lo, mix_u, mix_z, next_disp, u, z, v, w)
     return u_out.transpose(1, 0, 2), z_out.transpose(1, 0, 2), next_disp, wetted
 
 

time: 68.8 us -> 66.1 us (0.961)
  Pallas kernels: 67.3 us -> 65.1 us
    pallas_call x1, Pallas kernels: 54.5 us -> 52.9 us  [on_device(): pl.pallas_call(functools.partial(exchange_kernel, n_g, n_r), out_shape=(j...]
where the time goes in v3:
time: 66.1 us; the launch traced here: 65.9 us
  Pallas kernels  65.1 us (98%)
  between operations  0.8 us (1%)
    pallas_call x1, Pallas kernels, on_device(): pl.pallas_call(functools.partial(exchange_kernel, n_g, n_r), out_shape=(j...  52.9 us
    pallas_call x1, Pallas kernels, on_device(): pl.pallas_call(functools.partial(finish_kernel, n), out_shape=(jax.ShapeD...  12.2 us

profile of v3, /device:TPU:1, one launch (start us, length us, event | category | flops | bytes accessed | tf_op | source)
XLA Modules:
  0.0 65.9 jit_solution(14035750391323536433)
XLA Ops:
  0.6 52.9 %exchange.1 = (bf16[768,256]{1,0:T(8,128)(2,1)}, bf16[768,256]{1,0:T(8,128)(2,1)}, f32[192,256]{1,0:T(8,128)}, f32[192,256]{1,0:T(8,128)}, f32[6,256]{1,0:T(8,128)}) custom-call(f32[6,8192]{1,0:T(8,128)} %force.1, s32[1,8192]{1,0:T(1,128)} %bitcast.18, s32[1,8192]{1,0:T(1,128)} %bitcast.20, f32[256,256]{1,0:T(8,128)} %bitcast.17, f32[6,256]{1,0:T(8,128)} %disp_any.1, ...), custom_call_target="tpu_custom_call" | custom-call | tf_op jit(solution)/shard_map/exchange/pallas_call | solution.py:427
  53.5 12.2 %finish.1 = (f32[6,192,256]{2,1,0:T(8,128)}, f32[6,192,256]{2,1,0:T(8,128)}, f32[6,256]{1,0:T(8,128)}, f32[6,8192]{1,0:T(8,128)}) custom-call(s32[1,8192]{1,0:T(1,128)} %bitcast.19, s32[1,8192]{1,0:T(1,128)} %bitcast.21, bf16[768,256]{1,0:T(8,128)(2,1)} %get-tuple-element.13.table_hi, bf16[768,256]{1,0:T(8,128)(2,1)} %get-tuple-element.14.table_lo, ...), custom_call_target="tpu_custom_call" | custom-call | tf_op jit(solution)/shard_map/finish/pallas_call | solution.py:466
